TPU v7x, 512 devices: a whole 4x4x16 slice. The times are simulated.
512 devices in a mesh: vocab: 16 (over z_hi, y, core), dp: 8 (over z_lo), replica: 4 (over x).
Axes of the slice: x: 4, y: 4, z: 16 (z_hi: 2, z_lo: 8; z = z_hi * 8 + z_lo), core: 2. Of those that a mesh axis runs over, the one named last changes fastest.
Arguments:
- hidden: bfloat16 [1024, 4096], P('dp'), may hold values from -6 to 6
- head_weight: bfloat16 [4096, 65536], P('dp', ('vocab', 'replica')), may hold values from -0.09375 to 0.09375
- head_bias: float32 [65536], P(('vocab', 'replica')), may hold values from -2.5 to 2.5
- rep_cotangent: float32 [64, 65536], P('dp', ('vocab', 'replica')), may hold values from -6 to 6
- lengths: int32 [64], P('dp'), may hold values from 1 to 16, 640 in all
Outputs:
- pooled: float32 [64, 65536], P('dp', ('vocab', 'replica'))
- term_mean: float32 [65536], P(('vocab', 'replica'))
- bias_grad: float32 [65536], P(('vocab', 'replica'))
- weight_grad: float32 [4096, 65536], P('dp', ('vocab', 'replica'))
- input_grad: float32 [1024, 4096], P(('vocab', 'replica'), 'dp')
Inputs may be any that keep to these rules, and one draw needn't show every extreme that they name: `lengths`: each sequence has at least one live token; some sequence has all 16 live.
All inputs are finite; a program needn't handle non-finite values. No bound on the sum of `lengths` on one device may be relied on, other than what follows from the above.
Results may differ from a plain program's by a relative error of at most 0.015.
Values may be sent and summed in bfloat16 or wider, within the bound.
No kernel may reach another device: no remote copies, remote signals or barrier semaphores. Data moves between devices by JAX's collectives and lax.ppermute only.
A program may use at most 64 MiB of HBM per device.

v0:
```python
import jax
import jax.numpy as jnp
from jax import lax
from jax.sharding import PartitionSpec as P


def per_device(hidden, head_weight, head_bias, rep_cotangent, lengths):
    tok_rows = hidden.shape[0]
    block = head_weight.shape[0]
    vocab_cols = head_weight.shape[1]
    dp_count = lax.axis_size("dp")
    seq_count = lengths.shape[0]
    seq_len = tok_rows // seq_count
    columns = lax.all_to_all(hidden, "dp", split_axis=1, concat_axis=0, tiled=True)
    running = jnp.zeros((tok_rows, vocab_cols), jnp.float32)
    piece = lax.all_gather(head_weight, "dp", axis=0, tiled=True)
    count = piece.shape[0] // block
    for index in range(count):
        left = lax.dynamic_slice_in_dim(hidden, index * block, block, 1)
        part = jnp.dot(
            left, piece[index * block : (index + 1) * block, :], preferred_element_type=jnp.float32
        ).astype(jnp.bfloat16)
        running = running + lax.optimization_barrier(part).astype(jnp.float32)
    logits = running + head_bias[None, :]
    positive = jnp.maximum(logits, 0.0)
    grid = jnp.log1p(positive).reshape(seq_count, seq_len, vocab_cols)
    live = (jnp.arange(seq_len, dtype=jnp.int32)[None, :] < lengths[:, None]).astype(jnp.float32)[
        :, :, None
    ]
    squared = grid * grid
    total = 1.0 + jnp.sum(live * squared * squared, axis=1)
    pooled = total**0.25 - 1.0
    factor = (
        live
        * squared
        * grid
        * (total ** (-0.75))[:, None, :]
        / (1.0 + positive.reshape(seq_count, seq_len, vocab_cols))
    )
    column_sum = jnp.sum(pooled, axis=0)
    seq_total = seq_count * dp_count
    term_mean = lax.psum(column_sum, "dp") / seq_total
    grad_pooled = rep_cotangent + term_mean[None, :]
    grad_logits = (factor * grad_pooled[:, None, :]).reshape(tok_rows, vocab_cols)
    bias_grad = lax.psum(jnp.sum(grad_logits, axis=0), "dp")
    grad_round = grad_logits.astype(jnp.bfloat16)
    piece = lax.all_gather(grad_round, "dp", axis=0, tiled=True)
    left = columns
    weight_sum_acc = jnp.einsum("tk,tv->kv", left, piece, preferred_element_type=jnp.float32)
    rows_out = jnp.einsum("tv,kv->tk", piece, head_weight, preferred_element_type=jnp.float32)
    input_part = rows_out
    weight_grad, input_part = (weight_sum_acc, input_part)
    input_grad = lax.psum_scatter(input_part, ("vocab", "replica"), scatter_dimension=0, tiled=True)
    return (pooled, term_mean, bias_grad, weight_grad, input_grad)


def solution(mesh):
    placed = (
        P("dp", None),
        P("dp", ("vocab", "replica")),
        P(("vocab", "replica")),
        P("dp", ("vocab", "replica")),
        P("dp"),
    )
    return jax.shard_map(
        per_device,
        mesh=mesh,
        in_specs=placed,
        out_specs=(
            P("dp", ("vocab", "replica")),
            P(("vocab", "replica")),
            P(("vocab", "replica")),
            P("dp", ("vocab", "replica")),
            P(("vocab", "replica"), "dp"),
        ),
        check_vma=False,
    )
```

profile of v0, /device:TPU:64, one launch (start us, length us, event | category | flops | bytes accessed | tf_op | source)
XLA Modules:
  0.0 897.8 jit_solution(8657482168924879488)
XLA Ops:
  7.2 0.0 copy-start.3
  7.2 0.0 all-gather.3.cloned.1.call-start
  7.2 0.7 all-gather.3.cloned.1.call-update
  7.9 0.0 all-gather.5.cloned.1.call-start
  8.0 0.7 fusion.18
  8.7 0.1 reshape.55
  8.8 180.1 %all-gather.3.cloned.1.call-done = bf16[4096,1024]{1,0:T(8,128)(2,1)} async-done(((bf16[512,1024]{1,0:T(8,128)(2,1)}), bf16[4096,1024]{1,0:T(8,128)(2,1)}) %all-gather.3.cloned.1.call-update) | async-done | bytes 8388624 | tf_op jit(solution)/shard_map/all_gather | solution.py:16
  188.9 1.6 convolution_convert_fusion.7
  190.5 1.6 convolution_convert_fusion.6
  192.1 1.6 convolution_convert_fusion.5
  193.7 1.6 convolution_convert_fusion.4
  195.4 1.6 convolution_convert_fusion.3
  197.0 1.6 convolution_convert_fusion.2
  198.6 1.6 convolution_convert_fusion.1
  200.2 1.6 convolution_convert_fusion
  201.9 0.6 fusion.8
  202.5 0.6 fusion.20
  203.1 26.0 %psum.14 = f32[1024]{0:T(1024)S(1)} all-reduce(f32[1024]{0:T(1024)S(1)} %get-tuple-element.22), channel_id=1, replica_groups=mesh['vocab'=16,'dp'=8,'replica'=4] {'dp'}, use_global_device_ids=true, to_apply=%region_2.0 | all-reduce | flops 1024 | bytes 8192 | tf_op jit(solution)/shard_map/psum | solution.py:42
  229.1 0.0 copy-start.2
  229.1 1.0 fusion.19
  230.1 0.0 all-gather.5.cloned.1.call-update
  230.1 0.0 reduce-scatter.2.cloned.1.call-start
  230.2 73.2 %all-gather.5.cloned.1.call-done = bf16[1024,1024]{1,0:T(8,128)(2,1)} async-done(((bf16[128,1024]{1,0:T(8,128)(2,1)}), bf16[1024,1024]{1,0:T(8,128)(2,1)}) %all-gather.5.cloned.1.call-update) | async-done | bytes 2097168 | tf_op jit(solution)/shard_map/all_gather | solution.py:47
  303.4 4.2 fusion.21
  307.5 0.0 reduce-scatter.2.cloned.1.call-update
  307.6 1.6 copy.12
  309.2 59.9 %all_to_all.19 = bf16[128,8,512]{0,2,1:T(8,128)(2,1)S(1)} all-to-all(bf16[128,8,512]{0,2,1:T(8,128)(2,1)S(1)} %bitcast.22), channel_id=1, replica_groups=mesh['vocab'=16,'dp'=8,'replica'=4] {'dp'}, dimensions={1} | all-to-all | bytes 2097152 | tf_op jit(solution)/shard_map/all_to_all | solution.py:14
  369.1 0.5 copy.13
  369.7 23.8 %psum.15 = f32[1024]{0:T(1024)} all-reduce(f32[1024]{0:T(1024)S(1)} %reduce_sum.29), channel_id=1, replica_groups=mesh['vocab'=16,'dp'=8,'replica'=4] {'dp'}, use_global_device_ids=true, to_apply=%region_4.0 | all-reduce | flops 1024 | bytes 8192 | tf_op jit(solution)/shard_map/psum | solution.py:45
  393.5 2.9 convolution_bitcast_fusion
  396.4 1.8 copy.14
  398.2 493.1 %reduce-scatter.2.cloned.1.call-done = f32[16,512]{1,0:T(8,128)} async-done(((f32[1024,512]{1,0:T(8,128)}), f32[16,512]{1,0:T(8,128)}) %reduce-scatter.2.cloned.1.call-update) | async-done | bytes 32784 | tf_op jit(solution)/shard_map/reduce_scatter | solution.py:53
  (9 shorter events, 0.1 us)
Async XLA Ops:
  7.2 194.7 %copy-start.3 = (f32[1024]{0:T(1024)S(1)}, f32[1024]{0:T(1024)}, u32[]{:S(2)}) copy-start(f32[1024]{0:T(1024)} %param.7) | copy-start | bytes 12292
  7.2 221.9 %copy-start.1 = (f32[8,1024]{1,0:T(8,128)S(1)}, f32[8,1024]{1,0:T(8,128)}, u32[]{:S(2)}) copy-start(f32[8,1024]{1,0:T(8,128)} %param.8) | copy-start | bytes 98308
  7.2 181.7 %all-gather.3.cloned.1.call-start = ((), (), s32[]{:S(2)}) async-start(), calls=%async_computation.2 | async-start | bytes 9437184 | tf_op jit(solution)/shard_map/all_gather | solution.py:16
  7.9 295.4 %all-gather.5.cloned.1.call-start = ((), (), s32[]{:S(2)}) async-start(), calls=%async_computation.3 | async-start | bytes 2359296 | tf_op jit(solution)/shard_map/all_gather | solution.py:47
  8.8 294.6 %copy-start = (bf16[512,1024]{1,0:T(8,128)(2,1)S(1)}, bf16[512,1024]{1,0:T(8,128)(2,1)}, u32[]{:S(2)}) copy-start(bf16[512,1024]{1,0:T(8,128)(2,1)} %param.6) | copy-start | bytes 3145732
  229.1 140.0 %copy-start.2 = (f32[1024]{0:T(1024)}, f32[1024]{0:T(1024)S(1)}, u32[]{:S(2)}) copy-start(f32[1024]{0:T(1024)S(1)} %broadcast_multiply_fusion) | copy-start | bytes 12292
  230.1 661.1 %reduce-scatter.2.cloned.1.call-start = ((), (), s32[]{:S(2)}) async-start(), calls=%async_computation.4 | async-start | bytes 2129920 | tf_op jit(solution)/shard_map/reduce_scatter | solution.py:53
Sparse Core Ops, SparseCore 0:
  10.1 178.7 all-gather.2
  230.3 73.0 all-gather.4
  307.7 583.5 reduce-scatter.1
where the time goes:
time: 898 us
  waiting for transfers between devices  747 us (83%)
  blocking collectives  110 us (12%)
  matrix products  20 us (2%)
  between operations  13.9 us (2%)
    reduce_scatter x1, waiting for transfers between devices, per_device(): lax.psum_scatter(input_part, ('vocab', 'replica'), scatter_dimension=0, t...  493 us
    all_gather x1, waiting for transfers between devices, per_device(): piece = lax.all_gather(head_weight, 'dp', axis=0, tiled=True)  180 us
    all_gather x1, waiting for transfers between devices, per_device(): piece = lax.all_gather(grad_round, 'dp', axis=0, tiled=True)  73.2 us
    all_to_all x1, blocking collectives, per_device(): lax.all_to_all(hidden, 'dp', split_axis=1, concat_axis=0, tiled=True)  59.9 us
    psum x1, blocking collectives, per_device(): term_mean = lax.psum(column_sum, 'dp') / seq_total  26 us
    psum x1, blocking collectives, per_device(): bias_grad = lax.psum(jnp.sum(grad_logits, axis=0), 'dp')  23.8 us
  transfers between devices with their start and end apart: 3, of which 3 were waited for; matrix products, arithmetic and copies ran while one was open for 1% of the time, Pallas kernels for 0%

commit v1 on v0

--- a/solution.py
+++ b/solution.py
@@ -44,7 +44,9 @@
     grad_logits = (factor * grad_pooled[:, None, :]).reshape(tok_rows, vocab_cols)
     bias_grad = lax.psum(jnp.sum(grad_logits, axis=0), "dp")
     grad_round = grad_logits.astype(jnp.bfloat16)
-    piece = lax.all_gather(grad_round, "dp", axis=0, tiled=True)
+    piece = jnp.concatenate(
+        lax.all_to_all(jnp.stack([grad_round] * lax.axis_size("dp")), "dp", 0, 0), axis=0
+    )
     left = columns
     weight_sum_acc = jnp.einsum("tk,tv->kv", left, piece, preferred_element_type=jnp.float32)
     rows_out = jnp.einsum("tv,kv->tk", piece, head_weight, preferred_element_type=jnp.float32)

time: 898 us -> 935 us (1.041)
  the two profiles are of different devices: /device:TPU:64 before, /device:TPU:160 now
where the time goes in v1:
time: 935 us; the launch traced here: 934 us
  waiting for transfers between devices  699 us (75%)
  blocking collectives  177 us (19%)
  matrix products  19.8 us (2%)
  between operations  14.2 us (2%)
  starting transfers between devices  10.7 us (1%)
    reduce_scatter x1, waiting for transfers between devices, per_device(): lax.psum_scatter(input_part, ('vocab', 'replica'), scatter_dimension=0, t...  519 us
    all_gather x1, waiting for transfers between devices, per_device(): piece = lax.all_gather(head_weight, 'dp', axis=0, tiled=True)  180 us
    all_to_all x1, blocking collectives, per_device(): lax.all_to_all(jnp.stack([grad_round] * lax.axis_size('dp')), 'dp', 0, 0)  103 us
    psum x1, blocking collectives, per_device(): bias_grad = lax.psum(jnp.sum(grad_logits, axis=0), 'dp')  55.8 us
  transfers between devices with their start and end apart: 3, of which 2 were waited for; matrix products, arithmetic and copies ran while one was open for 1% of the time, Pallas kernels for 0%

profile of v1, /device:TPU:160, one launch (start us, length us, event | category | flops | bytes accessed | tf_op | source)
XLA Modules:
  0.0 934.3 jit_solution(10259096070349075655)
XLA Ops:
  7.2 0.0 all-gather.2.cloned.1.call-start
  7.2 0.7 all-gather.2.cloned.1.call-update
  7.9 0.0 reduce-scatter.2.cloned.1.call-start
  8.0 0.7 fusion.19
  8.7 0.1 reshape.61
  8.8 180.0 %all-gather.2.cloned.1.call-done = bf16[4096,1024]{1,0:T(8,128)(2,1)} async-done(((bf16[512,1024]{1,0:T(8,128)(2,1)}), bf16[4096,1024]{1,0:T(8,128)(2,1)}) %all-gather.2.cloned.1.call-update) | async-done | bytes 8388624 | tf_op jit(solution)/shard_map/all_gather | solution.py:16
  188.8 1.6 convolution_convert_fusion.7
  190.4 1.6 convolution_convert_fusion.6
  192.1 1.6 convolution_convert_fusion.5
  193.7 1.6 convolution_convert_fusion.4
  195.3 1.6 convolution_convert_fusion.3
  196.9 1.6 convolution_convert_fusion.2
  198.6 1.6 convolution_convert_fusion.1
  200.2 1.7 convolution_convert_fusion
  201.9 0.6 fusion.9
  202.5 0.6 fusion.21
  203.1 18.7 %psum.14 = f32[1024]{0:T(1024)S(1)} all-reduce(f32[1024]{0:T(1024)S(1)} %get-tuple-element.17), channel_id=1, replica_groups=mesh['vocab'=16,'dp'=8,'replica'=4] {'dp'}, use_global_device_ids=true, to_apply=%region_2.0 | all-reduce | flops 1024 | bytes 8192 | tf_op jit(solution)/shard_map/psum | solution.py:42
  221.9 1.1 fusion.20
  223.0 0.2 copy.12
  223.1 0.3 stack.2
  223.4 102.7 %all_to_all.21 = bf16[8,128,1024]{1,2,0:T(8,128)(2,1)S(1)} all-to-all(bf16[8,128,1024]{1,2,0:T(8,128)(2,1)S(1)} %stack.2), channel_id=1, replica_groups=mesh['vocab'=16,'dp'=8,'replica'=4] {'dp'}, dimensions={0} | all-to-all | bytes 4194304 | tf_op jit(solution)/shard_map/all_to_all | solution.py:48
  326.1 2.6 copy.15
  328.7 4.2 fusion.22
  332.9 0.0 reduce-scatter.2.cloned.1.call-update
  332.9 1.6 copy.13
  334.6 1.3 copy.14
  335.9 10.6 %all-to-all-start.1 = ((bf16[128,8,512]{2,0,1:T(8,128)(2,1)}), bf16[128,8,512]{2,0,1:T(8,128)(2,1)S(1)}, u32[]{:S(2)}, u32[]{:S(2)}) async-start(bf16[128,8,512]{2,0,1:T(8,128)(2,1)} %copy.14), calls=%async_computation.1 | async-start | bytes 2097152 | tf_op jit(solution)/shard_map/all_to_all | solution.py:14
  346.5 1.1 reduce_sum.29
  347.6 55.8 %psum.15 = f32[1024]{0:T(1024)} all-reduce(f32[1024]{0:T(1024)S(1)} %reduce_sum.29), channel_id=1, replica_groups=mesh['vocab'=16,'dp'=8,'replica'=4] {'dp'}, use_global_device_ids=true, to_apply=%region_4.0 | all-reduce | flops 1024 | bytes 8192 | tf_op jit(solution)/shard_map/psum | solution.py:45
  403.4 2.5 convolution_bitcast_fusion
  405.9 2.9 copy.16
  408.8 518.7 %reduce-scatter.2.cloned.1.call-done = f32[16,512]{1,0:T(8,128)} async-done(((f32[1024,512]{1,0:T(8,128)}), f32[16,512]{1,0:T(8,128)}) %reduce-scatter.2.cloned.1.call-update) | async-done | bytes 32784 | tf_op jit(solution)/shard_map/reduce_scatter | solution.py:55
  (11 shorter events, 0.0 us)
Async XLA Ops:
  7.2 194.7 %copy-start.3 = (f32[1024]{0:T(1024)S(1)}, f32[1024]{0:T(1024)}, u32[]{:S(2)}) copy-start(f32[1024]{0:T(1024)} %param.7) | copy-start | bytes 12292
  7.2 214.7 %copy-start.1 = (f32[8,1024]{1,0:T(8,128)S(1)}, f32[8,1024]{1,0:T(8,128)}, u32[]{:S(2)}) copy-start(f32[8,1024]{1,0:T(8,128)} %param.8) | copy-start | bytes 98308
  7.2 181.6 %all-gather.2.cloned.1.call-start = ((), (), s32[]{:S(2)}) async-start(), calls=%async_computation.3 | async-start | bytes 9437184 | tf_op jit(solution)/shard_map/all_gather | solution.py:16
  7.9 919.6 %reduce-scatter.2.cloned.1.call-start = ((), (), s32[]{:S(2)}) async-start(), calls=%async_computation.4 | async-start | bytes 2129920 | tf_op jit(solution)/shard_map/reduce_scatter | solution.py:55
  200.2 128.5 %copy-start = (bf16[512,1024]{1,0:T(8,128)(2,1)S(1)}, bf16[512,1024]{1,0:T(8,128)(2,1)}, u32[]{:S(2)}) copy-start(bf16[512,1024]{1,0:T(8,128)(2,1)} %param.6) | copy-start | bytes 3145732
  221.9 111.1 %copy-start.2 = (f32[1024]{0:T(1024)}, f32[1024]{0:T(1024)S(1)}, u32[]{:S(2)}) copy-start(f32[1024]{0:T(1024)S(1)} %broadcast_multiply_fusion) | copy-start | bytes 12292
  335.9 67.5 %all-to-all-start.1 = ((bf16[128,8,512]{2,0,1:T(8,128)(2,1)}), bf16[128,8,512]{2,0,1:T(8,128)(2,1)S(1)}, u32[]{:S(2)}, u32[]{:S(2)}) async-start(bf16[128,8,512]{2,0,1:T(8,128)(2,1)} %copy.14), calls=%async_computation.1 | async-start | bytes 2097152 | tf_op jit(solution)/shard_map/all_to_all | solution.py:14
Sparse Core Ops, SparseCore 0:
  10.1 178.6 all-gather.1
  333.1 594.3 reduce-scatter.1
